TPU v7x, 512 devices: a whole 4x4x16 slice. The times are simulated.
512 devices in a mesh: wide: 64 (over z, y_hi, core), narrow: 8 (over y_lo, x).
Axes of the slice: x: 4, y: 4 (y_hi: 2, y_lo: 2; y = y_hi * 2 + y_lo), z: 16, core: 2. Of those that a mesh axis runs over, the one named last changes fastest.
Arguments:
- offsets: float32 [3, 64, 8, 512], P(None, 'wide', 'narrow'), may hold values from 0 to 1
- bases: int32 [3, 64, 8, 512], P(None, 'wide', 'narrow'), may hold values from 0 to 511, as said below
- charges: float32 [64, 8, 512], P('wide', 'narrow'), may hold values from -4 to 4
- counts: int32 [64, 8], P('wide', 'narrow'), may hold values from 32 to 512, as said below
- cotangent: float32 [1], replicated, may hold values from 0.5 to 2
Outputs:
- forces: float32 [3, 64, 8, 512], P(None, 'wide', 'narrow')
- charge_grads: float32 [64, 8, 512], P('wide', 'narrow')
Inputs may be any that keep to these rules, and one draw needn't show every extreme that they name: `counts`: slots at or beyond a domain's count are padding; some domain holds exactly 512 atoms. `bases`: component 0 is below 4 and component 1 below 8 (the lowest stencil cell lies in the atom's own domain); component 2 is below 512.
All inputs are finite; a program needn't handle non-finite values.
Results may differ from a plain program's by a relative error of at most 0.0003.
Values sent between devices are 32-bit elements; how exact they have to be, the bound alone decides.
A program may use at most 64 MiB of HBM per device.

v0:
```python
import math
import jax
import jax.numpy as jnp
from jax import lax
from jax.sharding import PartitionSpec as P

CX = 4
CY = 8
NZ = 512
PRECISE = lax.Precision.HIGHEST
splitting_width = 1.0
block_limit = 512


def from_behind(block, axis, distance):
    devices = range(lax.axis_size(axis))
    route = [((i - distance) % len(devices), i) for i in devices]
    return lax.ppermute(block, axis, route)


def spline_pair(offset):
    rest = 1.0 - offset
    square = offset * offset
    cube = square * offset
    weights = jnp.stack(
        [
            rest * rest * rest / 6.0,
            (3.0 * cube - 6.0 * square + 4.0) / 6.0,
            (-3.0 * cube + 3.0 * square + 3.0 * offset + 1.0) / 6.0,
            cube / 6.0,
        ],
        axis=1,
    )
    slopes = jnp.stack(
        [
            -0.5 * rest * rest,
            1.5 * square - 2.0 * offset,
            -1.5 * square + offset + 0.5,
            0.5 * square,
        ],
        axis=1,
    )
    return (weights, slopes)


def wave_terms(wave_index, length):
    signed = (
        jnp.where(2 * wave_index < length, wave_index, wave_index - length).astype(jnp.float32)
        / length
    )
    phase_angle = (wave_index % length).astype(jnp.float32) * (2.0 * math.pi / length)
    spline = 9.0 / (2.0 + jnp.cos(phase_angle)) ** 2
    return (signed * signed, spline)


def influence(wave_x, wave_y, wave_z, size_x, size_y, size_z):
    square_x, spline_x = wave_terms(wave_x, size_x)
    square_y, spline_y = wave_terms(wave_y, size_y)
    square_z, spline_z = wave_terms(wave_z, size_z)
    squared = square_x + square_y + square_z
    positive = jnp.where(squared > 0.0, squared, 1.0)
    volume = float(size_x * size_y * size_z)
    kernel = jnp.exp(-math.pi**2 * squared / (splitting_width * splitting_width)) / (
        math.pi * volume * positive
    )
    kernel = kernel * spline_x * spline_y * spline_z
    return jnp.where(squared > 0.0, kernel, 0.0)


def dft_tables(length, sign):
    wave = jnp.arange(length, dtype=jnp.int32)
    phase = wave[:, None] * wave[None, :] % length
    phase_angle = phase.astype(jnp.float32) * (2.0 * math.pi / length)
    return (jnp.cos(phase_angle), sign * jnp.sin(phase_angle))


def rotation_matrix(width):
    row_ids = jnp.arange(width, dtype=jnp.int32)[:, None]
    column_ids = jnp.arange(width, dtype=jnp.int32)[None, :]
    raise_part = ((row_ids % 2 == 0) & (column_ids == row_ids + 1)).astype(jnp.float32)
    lower_part = ((row_ids % 2 == 1) & (column_ids == row_ids - 1)).astype(jnp.float32)
    return raise_part - lower_part


def complex_dft(values, cosine_table, sine_table, rotation, einsum_form):
    real_term = jnp.einsum(einsum_form, cosine_table, values, precision=PRECISE)
    turned = jnp.einsum(einsum_form, sine_table, values, precision=PRECISE)
    return real_term + jnp.dot(turned, rotation, precision=PRECISE)


def axis_table(cells, corner_row, values, wrap):
    cell_ids = jnp.arange(cells, dtype=jnp.int32)[:, None]
    table = jnp.zeros((cells, corner_row.shape[0]), jnp.float32)
    for step_index in range(4):
        target = corner_row + step_index
        if wrap:
            target = target % cells
        table = table + jnp.where(cell_ids == target[None, :], values[step_index][None, :], 0.0)
    return table


def spread_atoms(running, fraction, corner, charge, ext_rows, depth):
    ext_planes = running.shape[0] // (ext_rows * depth)
    weights = spline_pair(fraction)[0]
    plane_table = axis_table(ext_planes, corner[0], weights[0], False)
    row_table = axis_table(ext_rows, corner[1], weights[1], False)
    depth_table = axis_table(depth, corner[2], weights[2], True)
    cross = (plane_table[:, None, :] * row_table[None, :, :] * charge[None, None, :]).reshape(
        ext_planes * ext_rows, -1
    )
    grid = lax.dot_general(cross, depth_table, (((1,), (1,)), ((), ())), precision=PRECISE)
    return running + grid.reshape(-1)


def interpolate(fraction, corner, charge, occupied, potential_flat, ext_rows, depth, factor):
    ext_planes = potential_flat.shape[0] // (ext_rows * depth)
    weights, slopes = spline_pair(fraction)
    plane_w = axis_table(ext_planes, corner[0], weights[0], False)
    plane_s = axis_table(ext_planes, corner[0], slopes[0], False)
    row_w = axis_table(ext_rows, corner[1], weights[1], False)
    row_s = axis_table(ext_rows, corner[1], slopes[1], False)
    depth_w = axis_table(depth, corner[2], weights[2], True)
    depth_s = axis_table(depth, corner[2], slopes[2], True)
    potential_grid = potential_flat.reshape(ext_planes * ext_rows, depth)
    along_w = jnp.dot(potential_grid, depth_w, precision=PRECISE).reshape(ext_planes, ext_rows, -1)
    along_s = jnp.dot(potential_grid, depth_s, precision=PRECISE).reshape(ext_planes, ext_rows, -1)
    rows_ww = jnp.sum(row_w[None, :, :] * along_w, axis=1)
    rows_sw = jnp.sum(row_s[None, :, :] * along_w, axis=1)
    rows_ws = jnp.sum(row_w[None, :, :] * along_s, axis=1)
    potential_sum = jnp.sum(plane_w * rows_ww, axis=0)
    pull_x = jnp.sum(plane_s * rows_ww, axis=0)
    pull_y = jnp.sum(plane_w * rows_sw, axis=0)
    pull_z = jnp.sum(plane_w * rows_ws, axis=0)
    grads = factor * occupied * potential_sum
    pulls = -factor * charge[None] * jnp.stack([pull_x, pull_y, pull_z])
    return (grads, pulls)


def on_device(offsets, bases, charges, counts, cotangent):
    wide_count = lax.axis_size("wide")
    narrow_count = lax.axis_size("narrow")
    slots = charges.shape[2]
    ext_planes = CX + 3
    ext_rows = CY + 3
    grid_x = CX * wide_count
    grid_y = CY * narrow_count
    row_share = grid_y // wide_count
    fraction = offsets[:, 0, 0, :]
    corner = bases[:, 0, 0, :]
    occupied = (jnp.arange(slots, dtype=jnp.int32) < counts[0, 0]).astype(jnp.float32)
    charge = charges[0, 0] * occupied
    factor = cotangent[0]
    size_block = math.gcd(slots, block_limit)
    cell_count = ext_planes * ext_rows * NZ

    def spread_all(block_index, running):
        return spread_atoms(running, fraction, corner, charge, ext_rows, NZ)

    flat_grid = lax.fori_loop(
        0, slots // size_block, spread_all, jnp.zeros((cell_count,), jnp.float32)
    )
    charge_grid = flat_grid.reshape(ext_planes, ext_rows, NZ)
    z_cosine, z_sine = dft_tables(NZ, -1.0)
    forward_z = jnp.stack([z_cosine, z_sine], axis=2).reshape(NZ, 2 * NZ)
    inverse_z = jnp.stack([z_cosine, z_sine], axis=1).reshape(2 * NZ, NZ)
    spectrum_width = 2 * NZ
    length = spectrum_width // narrow_count
    freq_share = length // 2
    rotation = rotation_matrix(length)
    y_cosine, y_sine = dft_tables(grid_y, -1.0)
    x_cosine, x_sine = dft_tables(grid_x, -1.0)
    planes_in = from_behind(charge_grid[CX:], "wide", 1)
    charge_grid = charge_grid[:CX].at[:3].add(planes_in)
    rows_in = from_behind(charge_grid[:, CY:], "narrow", 1)
    charge_grid = charge_grid[:, :CY].at[:, :3].add(rows_in)
    z_spectrum = jnp.dot(charge_grid.reshape(CX * CY, NZ), forward_z, precision=PRECISE).reshape(
        CX, CY, spectrum_width
    )
    columns = lax.all_to_all(z_spectrum, "narrow", split_axis=2, concat_axis=1, tiled=True)
    columns = complex_dft(columns, y_cosine, y_sine, rotation, "kn,pnl->pkl")
    spectrum = lax.all_to_all(columns, "wide", split_axis=1, concat_axis=0, tiled=True)
    spectrum = complex_dft(spectrum, x_cosine, x_sine, rotation, "kn,nrl->krl")
    wave_x = jnp.arange(grid_x, dtype=jnp.int32)[:, None, None]
    wave_y = (
        lax.axis_index("wide") * row_share + jnp.arange(row_share, dtype=jnp.int32)[None, :, None]
    )
    wave_z = (
        lax.axis_index("narrow") * freq_share
        + jnp.arange(freq_share, dtype=jnp.int32)[None, None, :]
    )
    kernel = influence(wave_x, wave_y, wave_z, grid_x, grid_y, NZ)
    filtered = spectrum * jnp.repeat(kernel, 2, axis=2)
    spectrum = complex_dft(filtered, x_cosine, -x_sine, rotation, "kn,nrl->krl")
    columns = lax.all_to_all(spectrum, "wide", split_axis=0, concat_axis=1, tiled=True)
    columns = complex_dft(columns, y_cosine, -y_sine, rotation, "kn,pnl->pkl")
    returned = lax.all_to_all(columns, "narrow", split_axis=1, concat_axis=2, tiled=True)
    potential = jnp.dot(
        returned.reshape(CX * CY, spectrum_width), inverse_z, precision=PRECISE
    ).reshape(CX, CY, NZ)
    upper_planes = from_behind(potential[:3], "wide", -1)
    potential = jnp.concatenate([potential, upper_planes], axis=0)
    side_rows = from_behind(potential[:, :3], "narrow", -1)
    potential = jnp.concatenate([potential, side_rows], axis=1)
    potential_flat = potential.reshape(-1)

    def read_block(block_index, results):
        grads_part, pulls_part = interpolate(
            fraction, corner, charge, occupied, potential_flat, ext_rows, NZ, factor
        )
        return (grads_part, pulls_part)

    start_results = (jnp.zeros((slots,), jnp.float32), jnp.zeros((3, slots), jnp.float32))
    grads, pulls = lax.fori_loop(0, slots // size_block, read_block, start_results)
    return (pulls.reshape(3, 1, 1, slots), grads.reshape(1, 1, slots))


def solution(mesh):
    placed = (
        P(None, "wide", "narrow", None),
        P(None, "wide", "narrow", None),
        P("wide", "narrow", None),
        P("wide", "narrow"),
        P(),
    )
    return jax.shard_map(
        on_device,
        mesh=mesh,
        in_specs=placed,
        out_specs=(P(None, "wide", "narrow", None), P("wide", "narrow", None)),
        check_vma=False,
    )
```

profile of v0, /device:TPU:1, one launch (start us, length us, event | category | flops | bytes accessed | tf_op | source)
XLA Modules:
  0.0 146.2 jit_solution(6606350430928284395)
XLA Ops:
  0.6 0.7 multiply_multiply_fusion.1
  1.4 0.7 fusion.215
  2.9 0.7 compare_select_fusion.1
  3.6 1.5 %fusion.26 = f32[77,512]{1,0:T(8,128)S(1)} fusion(f32[512]{0:T(512)S(1)} %bitcast.217, s32[512]{0:T(512)S(1)} %get-tuple-element.120, f32[512]{0:T(512)S(1)} %bitcast.215, s32[512]{0:T(512)S(1)} %get-tuple-element.119, f32[512]{0:T(512)S(1)} %bitcast.213, s32[512]{0:T(512)S(1)} %get-tuple-element.118, f32[512]{0:T(512)S(1)} %bitcast.211, ...), kind=kOutput, calls=%fused_computation.50 | convolution fusion | flops 245144064 | bytes 333824 | tf_op jit(solution)/shard_map/while/body/eval_jaxpr/dot_general | solution.py:111
  5.2 6.2 %collective-permute-start = (f32[3,11,512]{2,1,0:T(8,128)S(1)}, f32[3,11,512]{2,1,0:T(8,128)S(1)}, u32[]{:S(2)}, u32[]{:S(2)}) collective-permute-start(f32[3,11,512]{2,1,0:T(8,128)S(1)} %slice.335), channel_id=1, source_target_pairs={{504,0},{0,8},{8,16},{16,24},{24,32},{32,40},{40,48},{48,56},{56,6... | collective-permute-start | bytes 202760 | tf_op jit(solution)/shard_map/ppermute | solution.py:18
  11.4 5.3 %sine_multiply_fusion.1 = (f32[512,512,1]{1,0,2:T(8,128)S(1)}, f32[512,512,1]{1,0,2:T(8,128)}) fusion(), kind=kLoop, calls=%fused_computation.40 | loop fusion | flops 3932160 | bytes 2097152 | tf_op jit(solution)/shard_map/mul | solution.py:74
  16.8 3.1 %collective-permute-start.1 = (f32[4,3,512]{2,1,0:T(4,128)S(1)}, f32[4,3,512]{2,1,0:T(4,128)S(1)}, u32[]{:S(2)}, u32[]{:S(2)}) collective-permute-start(f32[4,3,512]{2,1,0:T(4,128)S(1)} %slice.371), channel_id=1, source_target_pairs={{7,0},{0,1},{1,2},{2,3},{3,4},{4,5},{5,6},{6,7},{15,8},{8,9},{9,10... | collective-permute-start | bytes 73736 | tf_op jit(solution)/shard_map/ppermute | solution.py:18
  20.0 1.4 pad_maximum_fusion
  21.4 2.5 %copy.38 = f32[512,512,2]{0,2,1:T(2,128)} copy(f32[512,512,2]{1,0,2:T(8,128)S(1)} %pad_maximum_fusion) | data formatting | bytes 4194304 | tf_op jit(solution)/shard_map/stack | solution.py:164
  23.8 2.7 %reshape.1289 = f32[512,1024]{0,1:T(8,128)S(1)} reshape(f32[512,512,2]{0,2,1:T(2,128)} %copy.38) | data formatting | bytes 4194304 | tf_op jit(solution)/shard_map/reshape | solution.py:164
  26.8 2.0 %fusion = f32[4,8,1024]{2,1,0:T(8,128)S(1)} fusion(f32[4,8,512]{2,1,0:T(8,128)S(1)} %scatter-add.9, f32[512,1024]{0,1:T(8,128)S(1)} %reshape.1289), kind=kOutput, calls=%fused_computation.2 | convolution fusion | flops 201326592 | bytes 2293760 | tf_op jit(solution)/shard_map/dot_general | solution.py:176
  28.8 0.8 copy.40
  29.6 3.1 %reshape.1301 = f32[8,1,4096]{2,1,0:T(1,128)} reshape(f32[1024,4,8]{2,1,0:T(4,128)S(1)} %bitcast.169) | data formatting | bytes 262144
  32.7 3.8 %all-to-all-start = ((f32[8,1,4096]{2,1,0:T(1,128)}), f32[8,1,4096]{2,1,0:T(1,128)S(1)}, u32[]{:S(2)}, u32[]{:S(2)}) async-start(f32[8,1,4096]{2,1,0:T(1,128)} %reshape.1301), calls=%async_computation | async-start | bytes 262144 | tf_op jit(solution)/shard_map/all_to_all | solution.py:179
  36.6 5.4 %all-to-all-done = f32[8,1,4096]{2,1,0:T(1,128)S(1)} async-done(((f32[8,1,4096]{2,1,0:T(1,128)}), f32[8,1,4096]{2,1,0:T(1,128)S(1)}, u32[]{:S(2)}, u32[]{:S(2)}) %all-to-all-start) | async-done | bytes 131104 | tf_op jit(solution)/shard_map/all_to_all | solution.py:179
  42.0 0.5 broadcast.1296
  42.5 1.0 reduce.4
  43.4 2.5 %reshape.1302 = f32[1024,4,8]{2,1,0:T(4,128)S(1)} reshape(f32[8,4096]{1,0:T(8,128)S(1)} %reduce.4) | data formatting | bytes 262144
  45.9 0.8 copy.41
  46.7 0.4 convolution_bitcast_fusion.2
  47.1 0.4 convolution_bitcast_fusion.3
  47.5 0.4 convolution_add_fusion.3
  47.9 0.7 copy.42
  48.6 18.5 %all-to-all-start.1 = ((f32[4,64,128]{2,0,1:T(4,128)}), f32[4,64,128]{2,0,1:T(4,128)S(1)}, u32[]{:S(2)}, u32[]{:S(2)}) async-start(f32[4,64,128]{2,0,1:T(4,128)} %copy.42), calls=%async_computation.1 | async-start | bytes 262144 | tf_op jit(solution)/shard_map/all_to_all | solution.py:181
  67.8 18.0 %all-to-all-done.1 = f32[4,64,128]{2,0,1:T(4,128)S(1)} async-done(((f32[4,64,128]{2,0,1:T(4,128)}), f32[4,64,128]{2,0,1:T(4,128)S(1)}, u32[]{:S(2)}, u32[]{:S(2)}) %all-to-all-start.1) | async-done | bytes 131104 | tf_op jit(solution)/shard_map/all_to_all | solution.py:181
  85.8 1.6 %fusion.64 = f32[256,128]{1,0:T(8,128)S(1)} fusion(f32[256,128]{1,0:T(8,128)S(1)} %bitcast.178), kind=kOutput, calls=%fused_computation.92 | convolution fusion | flops 101646336 | bytes 262144 | tf_op jit(solution)/shard_map/kn,nrl->krl/dot_general | solution.py:87
  87.7 1.6 %fusion.2 = f32[256,128]{1,0:T(8,128)S(1)} fusion(f32[256,128]{1,0:T(8,128)S(1)} %copy.43, f32[256,128]{1,0:T(8,128)S(1)} %fusion.93, f32[256,128]{1,0:T(8,128)S(1)} %bitcast.179), kind=kOutput, calls=%fused_computation.13 | convolution fusion | flops 101646336 | bytes 524288 | tf_op jit(solution)/shard_map/kn,nrl->krl/dot_general | solution.py:86
  89.3 1.6 %fusion.59 = f32[256,128]{1,0:T(8,128)S(1)} fusion(f32[256,128]{1,0:T(8,128)S(1)} %fusion.2), kind=kOutput, calls=%fused_computation.86 | convolution fusion | flops 101711872 | bytes 262144 | tf_op jit(solution)/shard_map/kn,nrl->krl/dot_general | solution.py:87
  90.8 0.4 fusion.92
  91.2 2.0 %convolution_add_fusion = f32[256,128]{1,0:T(8,128)} fusion(f32[256,128]{1,0:T(8,128)S(1)} %fusion.92, f32[256,128]{1,0:T(8,128)S(1)} %fusion.2), kind=kOutput, calls=%fused_computation.11 | convolution fusion | flops 101613568 | bytes 393216 | tf_op jit(solution)/shard_map/kn,nrl->krl/dot_general | solution.py:86
  93.2 4.4 %all-to-all-start.2 = ((f32[256,1,128]{2,1,0:T(1,128)}), f32[256,1,128]{2,1,0:T(1,128)S(1)}, u32[]{:S(2)}, u32[]{:S(2)}) async-start(f32[256,1,128]{2,1,0:T(1,128)} %bitcast.43), calls=%async_computation.2 | async-start | bytes 262144 | tf_op jit(solution)/shard_map/all_to_all | solution.py:194
  97.7 4.1 %sine_multiply_fusion = (f32[512,1,512]{2,0,1:T(8,128)S(1)}, f32[512,1,512]{2,0,1:T(8,128)S(1)}) fusion(), kind=kLoop, calls=%fused_computation.37 | loop fusion | flops 3932160 | bytes 2097152 | tf_op jit(solution)/shard_map/mul | solution.py:74
  101.8 14.6 %all-to-all-done.2 = f32[256,1,128]{2,1,0:T(1,128)S(1)} async-done(((f32[256,1,128]{2,1,0:T(1,128)}), f32[256,1,128]{2,1,0:T(1,128)S(1)}, u32[]{:S(2)}, u32[]{:S(2)}) %all-to-all-start.2) | async-done | bytes 131104 | tf_op jit(solution)/shard_map/all_to_all | solution.py:194
  116.4 0.4 convolution_bitcast_fusion
  116.8 0.4 convolution_bitcast_fusion.1
  117.6 0.7 copy.46
  118.3 3.6 %all-to-all-start.3 = ((f32[4,64,128]{2,0,1:T(4,128)}), f32[4,64,128]{2,0,1:T(4,128)S(1)}, u32[]{:S(2)}, u32[]{:S(2)}) async-start(f32[4,64,128]{2,0,1:T(4,128)} %copy.46), calls=%async_computation.3 | async-start | bytes 262144 | tf_op jit(solution)/shard_map/all_to_all | solution.py:196
  122.1 3.0 %copy.48 = f32[512,2,512]{2,1,0:T(2,128)} copy(f32[512,2,512]{2,0,1:T(8,128)S(1)} %pad_maximum_fusion.1) | data formatting | bytes 4194304 | tf_op jit(solution)/shard_map/stack | solution.py:165
  125.0 2.7 %reshape.1292 = f32[1024,512]{1,0:T(8,128)S(1)} reshape(f32[512,2,512]{2,1,0:T(2,128)} %copy.48) | data formatting | bytes 4194304 | tf_op jit(solution)/shard_map/reshape | solution.py:165
  127.9 1.3 fusion.66
  129.2 2.7 %collective-permute-start.2 = (f32[3,8,512]{2,1,0:T(8,128)S(1)}, f32[3,8,512]{2,1,0:T(8,128)S(1)}, u32[]{:S(2)}, u32[]{:S(2)}) collective-permute-start(f32[3,8,512]{2,1,0:T(8,128)S(1)} %slice_bitcast_fusion), channel_id=1, source_target_pairs={{8,0},{16,8},{24,16},{32,24},{40,32},{48,40},{56,48},{64,56},{72,6... | collective-permute-start | bytes 147464 | tf_op jit(solution)/shard_map/ppermute | solution.py:18
  132.6 3.5 %collective-permute-done.2 = f32[3,8,512]{2,1,0:T(8,128)S(1)} collective-permute-done((f32[3,8,512]{2,1,0:T(8,128)S(1)}, f32[3,8,512]{2,1,0:T(8,128)S(1)}, u32[]{:S(2)}, u32[]{:S(2)}) %collective-permute-start.2) | collective-permute-done | bytes 49184 | tf_op jit(solution)/shard_map/ppermute | solution.py:18
  136.1 5.2 %collective-permute-start.3 = (f32[7,3,512]{2,1,0:T(4,128)S(1)}, f32[7,3,512]{2,1,0:T(4,128)S(1)}, u32[]{:S(2)}, u32[]{:S(2)}) collective-permute-start(f32[7,3,512]{2,1,0:T(4,128)S(1)} %pad_maximum_fusion.5), channel_id=1, source_target_pairs={{1,0},{2,1},{3,2},{4,3},{5,4},{6,5},{7,6},{0,7},{9,8},{10,9},{11,1... | collective-permute-start | bytes 129032 | tf_op jit(solution)/shard_map/ppermute | solution.py:18
  141.3 1.2 collective-permute-done.3
  142.5 1.2 multiply_reduce_fusion.1
  143.8 1.2 fusion.3
  145.0 0.6 fusion.144
  145.6 0.6 maximum_multiply_fusion
  (42 shorter events, 2.0 us)
Async XLA Ops:
  5.2 11.6 %collective-permute-start = (f32[3,11,512]{2,1,0:T(8,128)S(1)}, f32[3,11,512]{2,1,0:T(8,128)S(1)}, u32[]{:S(2)}, u32[]{:S(2)}) collective-permute-start(f32[3,11,512]{2,1,0:T(8,128)S(1)} %slice.335), channel_id=1, source_target_pairs={{504,0},{0,8},{8,16},{16,24},{24,32},{32,40},{40,48},{48,56},{56,6... | collective-permute-start | bytes 202760 | tf_op jit(solution)/shard_map/ppermute | solution.py:18
  16.8 9.7 %collective-permute-start.1 = (f32[4,3,512]{2,1,0:T(4,128)S(1)}, f32[4,3,512]{2,1,0:T(4,128)S(1)}, u32[]{:S(2)}, u32[]{:S(2)}) collective-permute-start(f32[4,3,512]{2,1,0:T(4,128)S(1)} %slice.371), channel_id=1, source_target_pairs={{7,0},{0,1},{1,2},{2,3},{3,4},{4,5},{5,6},{6,7},{15,8},{8,9},{9,10... | collective-permute-start | bytes 73736 | tf_op jit(solution)/shard_map/ppermute | solution.py:18
  32.7 9.3 %all-to-all-start = ((f32[8,1,4096]{2,1,0:T(1,128)}), f32[8,1,4096]{2,1,0:T(1,128)S(1)}, u32[]{:S(2)}, u32[]{:S(2)}) async-start(f32[8,1,4096]{2,1,0:T(1,128)} %reshape.1301), calls=%async_computation | async-start | bytes 262144 | tf_op jit(solution)/shard_map/all_to_all | solution.py:179
  48.6 37.1 %all-to-all-start.1 = ((f32[4,64,128]{2,0,1:T(4,128)}), f32[4,64,128]{2,0,1:T(4,128)S(1)}, u32[]{:S(2)}, u32[]{:S(2)}) async-start(f32[4,64,128]{2,0,1:T(4,128)} %copy.42), calls=%async_computation.1 | async-start | bytes 262144 | tf_op jit(solution)/shard_map/all_to_all | solution.py:181
  93.2 23.1 %all-to-all-start.2 = ((f32[256,1,128]{2,1,0:T(1,128)}), f32[256,1,128]{2,1,0:T(1,128)S(1)}, u32[]{:S(2)}, u32[]{:S(2)}) async-start(f32[256,1,128]{2,1,0:T(1,128)} %bitcast.43), calls=%async_computation.2 | async-start | bytes 262144 | tf_op jit(solution)/shard_map/all_to_all | solution.py:194
  118.3 9.5 %all-to-all-start.3 = ((f32[4,64,128]{2,0,1:T(4,128)}), f32[4,64,128]{2,0,1:T(4,128)S(1)}, u32[]{:S(2)}, u32[]{:S(2)}) async-start(f32[4,64,128]{2,0,1:T(4,128)} %copy.46), calls=%async_computation.3 | async-start | bytes 262144 | tf_op jit(solution)/shard_map/all_to_all | solution.py:196
  127.7 13.6 %copy-start = (f32[1,1,512]{2,1,0:T(1,128)S(1)}, f32[1,1,512]{2,1,0:T(1,128)}, u32[]{:S(2)}) copy-start(f32[1,1,512]{2,1,0:T(1,128)} %param.11) | copy-start | bytes 6148
  129.2 6.9 %collective-permute-start.2 = (f32[3,8,512]{2,1,0:T(8,128)S(1)}, f32[3,8,512]{2,1,0:T(8,128)S(1)}, u32[]{:S(2)}, u32[]{:S(2)}) collective-permute-start(f32[3,8,512]{2,1,0:T(8,128)S(1)} %slice_bitcast_fusion), channel_id=1, source_target_pairs={{8,0},{16,8},{24,16},{32,24},{40,32},{48,40},{56,48},{64,56},{72,6... | collective-permute-start | bytes 147464 | tf_op jit(solution)/shard_map/ppermute | solution.py:18
  136.1 6.4 %collective-permute-start.3 = (f32[7,3,512]{2,1,0:T(4,128)S(1)}, f32[7,3,512]{2,1,0:T(4,128)S(1)}, u32[]{:S(2)}, u32[]{:S(2)}) collective-permute-start(f32[7,3,512]{2,1,0:T(4,128)S(1)} %pad_maximum_fusion.5), channel_id=1, source_target_pairs={{1,0},{2,1},{3,2},{4,3},{5,4},{6,5},{7,6},{0,7},{9,8},{10,9},{11,1... | collective-permute-start | bytes 129032 | tf_op jit(solution)/shard_map/ppermute | solution.py:18
where the time goes:
time: 147 us; the launch traced here: 146 us
  starting transfers between devices  47.6 us (32%)
  waiting for transfers between devices  42.7 us (29%)
  local copies, waits for them, and re-layouts  21.3 us (14%)
  matrix products  17.1 us (12%)
  other arithmetic  15 us (10%)
  between operations  2.55 us (2%)
    all_to_all x1, starting transfers between devices, on_device(): lax.all_to_all(columns, 'wide', split_axis=1, concat_axis=0, tiled=True)  18.5 us
    all_to_all x1, waiting for transfers between devices, on_device(): lax.all_to_all(columns, 'wide', split_axis=1, concat_axis=0, tiled=True)  18 us
    ppermute x4, starting transfers between devices, from_behind(): return lax.ppermute(block, axis, route)  17.2 us
    all_to_all x1, waiting for transfers between devices, on_device(): lax.all_to_all(spectrum, 'wide', split_axis=0, concat_axis=1, tiled=True)  14.6 us
    mul x2, other arithmetic, dft_tables(): return (jnp.cos(phase_angle), sign * jnp.sin(phase_angle))  9.43 us
    unnamed x4, local copies, waits for them, and re-layouts  5.56 us
    all_to_all x1, waiting for transfers between devices, on_device(): lax.all_to_all(z_spectrum, 'narrow', split_axis=2, concat_axis=1, tiled=T...  5.42 us
    ppermute x4, waiting for transfers between devices, from_behind(): return lax.ppermute(block, axis, route)  4.74 us
  transfers between devices with their start and end apart: 8, of which 5 were waited for; matrix products, arithmetic and copies ran while one was open for 15% of the time, Pallas kernels for 0%

commit v1 on v0

--- a/solution.py
+++ b/solution.py
@@ -191,7 +191,10 @@
     kernel = influence(wave_x, wave_y, wave_z, grid_x, grid_y, NZ)
     filtered = spectrum * jnp.repeat(kernel, 2, axis=2)
     spectrum = complex_dft(filtered, x_cosine, -x_sine, rotation, "kn,nrl->krl")
-    columns = lax.all_to_all(spectrum, "wide", split_axis=0, concat_axis=1, tiled=True)
+    columns = jnp.concatenate(
+        lax.all_to_all(jnp.stack(jnp.split(spectrum, lax.axis_size("wide"), axis=0)), "wide", 0, 0),
+        axis=1,
+    )
     columns = complex_dft(columns, y_cosine, -y_sine, rotation, "kn,pnl->pkl")
     returned = lax.all_to_all(columns, "narrow", split_axis=1, concat_axis=2, tiled=True)
     potential = jnp.dot(

time: 147 us -> 184 us (1.25)
  local copies, waits for them, and re-layouts: 21.3 us -> 58.6 us
    unnamed x4 -> x67, local copies, waits for them, and re-layouts: 5.56 us -> 42.3 us
  transfers between devices with their start and end apart: 8 -> 8, of which waited for: 5 -> 5; matrix products, arithmetic and copies ran while one was open for 15% -> 12% of each run, Pallas kernels for 0% -> 0%
where the time goes in v1:
time: 184 us; the launch traced here: 183 us
  local copies, waits for them, and re-layouts  58.6 us (32%)
  starting transfers between devices  47.7 us (26%)
  waiting for transfers between devices  42.7 us (23%)
  matrix products  16.6 us (9%)
  other arithmetic  15 us (8%)
  between operations  2.59 us (1%)
    unnamed x67, local copies, waits for them, and re-layouts  42.3 us
    all_to_all x1, starting transfers between devices, on_device(): lax.all_to_all(columns, 'wide', split_axis=1, concat_axis=0, tiled=True)  18.5 us
    all_to_all x1, waiting for transfers between devices, on_device(): lax.all_to_all(columns, 'wide', split_axis=1, concat_axis=0, tiled=True)  18 us
    ppermute x4, starting transfers between devices, from_behind(): return lax.ppermute(block, axis, route)  17.3 us
    all_to_all x1, waiting for transfers between devices, on_device(): lax.all_to_all(jnp.stack(jnp.split(spectrum, lax.axis_size('wide'), axis=...  14.6 us
    mul x2, other arithmetic, dft_tables(): return (jnp.cos(phase_angle), sign * jnp.sin(phase_angle))  9.43 us
    all_to_all x1, waiting for transfers between devices, on_device(): lax.all_to_all(z_spectrum, 'narrow', split_axis=2, concat_axis=1, tiled=T...  5.42 us
    ppermute x4, waiting for transfers between devices, from_behind(): return lax.ppermute(block, axis, route)  4.73 us
  transfers between devices with their start and end apart: 8, of which 5 were waited for; matrix products, arithmetic and copies ran while one was open for 12% of the time, Pallas kernels for 0%

profile of v1, /device:TPU:1, one launch (start us, length us, event | category | flops | bytes accessed | tf_op | source)
XLA Modules:
  0.0 183.1 jit_solution(13095808465757648184)
XLA Ops:
  0.6 0.7 multiply_multiply_fusion.1
  1.4 0.7 fusion.213
  2.9 0.7 compare_select_fusion.1
  3.6 1.5 fusion.26
  5.2 6.2 %collective-permute-start = (f32[3,11,512]{2,1,0:T(8,128)S(1)}, f32[3,11,512]{2,1,0:T(8,128)S(1)}, u32[]{:S(2)}, u32[]{:S(2)}) collective-permute-start(f32[3,11,512]{2,1,0:T(8,128)S(1)} %slice.399), channel_id=1, source_target_pairs={{504,0},{0,8},{8,16},{16,24},{24,32},{32,40},{40,48},{48,56},{56,6... | collective-permute-start | bytes 202760 | tf_op jit(solution)/shard_map/ppermute | solution.py:18
  11.4 5.3 %sine_multiply_fusion.1 = (f32[512,512,1]{1,0,2:T(8,128)S(1)}, f32[512,512,1]{1,0,2:T(8,128)}) fusion(), kind=kLoop, calls=%fused_computation.40 | loop fusion | flops 3932160 | bytes 2097152 | tf_op jit(solution)/shard_map/mul | solution.py:74
  16.8 3.1 %collective-permute-start.1 = (f32[4,3,512]{2,1,0:T(4,128)S(1)}, f32[4,3,512]{2,1,0:T(4,128)S(1)}, u32[]{:S(2)}, u32[]{:S(2)}) collective-permute-start(f32[4,3,512]{2,1,0:T(4,128)S(1)} %slice.435), channel_id=1, source_target_pairs={{7,0},{0,1},{1,2},{2,3},{3,4},{4,5},{5,6},{6,7},{15,8},{8,9},{9,10... | collective-permute-start | bytes 73736 | tf_op jit(solution)/shard_map/ppermute | solution.py:18
  20.0 1.4 pad_maximum_fusion
  21.4 2.5 %copy.39 = f32[512,512,2]{0,2,1:T(2,128)} copy(f32[512,512,2]{1,0,2:T(8,128)S(1)} %pad_maximum_fusion) | data formatting | bytes 4194304 | tf_op jit(solution)/shard_map/stack | solution.py:164
  23.8 2.7 %reshape.1423 = f32[512,1024]{0,1:T(8,128)S(1)} reshape(f32[512,512,2]{0,2,1:T(2,128)} %copy.39) | data formatting | bytes 4194304 | tf_op jit(solution)/shard_map/reshape | solution.py:164
  26.8 2.0 %fusion = f32[4,8,1024]{2,1,0:T(8,128)S(1)} fusion(f32[4,8,512]{2,1,0:T(8,128)S(1)} %scatter-add.9, f32[512,1024]{0,1:T(8,128)S(1)} %reshape.1423), kind=kOutput, calls=%fused_computation.2 | convolution fusion | flops 201326592 | bytes 2293760 | tf_op jit(solution)/shard_map/dot_general | solution.py:176
  28.8 0.8 copy.41
  29.6 3.1 %reshape.1437 = f32[8,1,4096]{2,1,0:T(1,128)} reshape(f32[1024,4,8]{2,1,0:T(4,128)S(1)} %bitcast.417) | data formatting | bytes 262144
  32.7 3.8 %all-to-all-start = ((f32[8,1,4096]{2,1,0:T(1,128)}), f32[8,1,4096]{2,1,0:T(1,128)S(1)}, u32[]{:S(2)}, u32[]{:S(2)}) async-start(f32[8,1,4096]{2,1,0:T(1,128)} %reshape.1437), calls=%async_computation | async-start | bytes 262144 | tf_op jit(solution)/shard_map/all_to_all | solution.py:179
  36.6 5.4 %all-to-all-done = f32[8,1,4096]{2,1,0:T(1,128)S(1)} async-done(((f32[8,1,4096]{2,1,0:T(1,128)}), f32[8,1,4096]{2,1,0:T(1,128)S(1)}, u32[]{:S(2)}, u32[]{:S(2)}) %all-to-all-start) | async-done | bytes 131104 | tf_op jit(solution)/shard_map/all_to_all | solution.py:179
  42.5 1.0 reduce.4
  43.4 2.5 %reshape.1438 = f32[1024,4,8]{2,1,0:T(4,128)S(1)} reshape(f32[8,4096]{1,0:T(8,128)S(1)} %reduce.4) | data formatting | bytes 262144
  45.9 0.8 copy.42
  47.9 0.7 copy.43
  48.6 18.5 %all-to-all-start.1 = ((f32[4,64,128]{2,0,1:T(4,128)}), f32[4,64,128]{2,0,1:T(4,128)S(1)}, u32[]{:S(2)}, u32[]{:S(2)}) async-start(f32[4,64,128]{2,0,1:T(4,128)} %copy.43), calls=%async_computation.1 | async-start | bytes 262144 | tf_op jit(solution)/shard_map/all_to_all | solution.py:181
  67.8 18.0 %all-to-all-done.1 = f32[4,64,128]{2,0,1:T(4,128)S(1)} async-done(((f32[4,64,128]{2,0,1:T(4,128)}), f32[4,64,128]{2,0,1:T(4,128)S(1)}, u32[]{:S(2)}, u32[]{:S(2)}) %all-to-all-start.1) | async-done | bytes 131104 | tf_op jit(solution)/shard_map/all_to_all | solution.py:181
  85.8 1.6 fusion.64
  87.7 1.6 fusion.2
  89.3 1.6 fusion.59
  91.2 1.6 convolution_add_fusion
  92.8 0.6 constant_dynamic-update-slice_fusion.63
  99.2 0.6 constant_dynamic-update-slice_fusion.52
  104.5 0.6 constant_dynamic-update-slice_fusion.43
  105.6 0.6 constant_dynamic-update-slice_fusion.41
  110.3 0.6 constant_dynamic-update-slice_fusion.33
  117.3 0.6 constant_dynamic-update-slice_fusion.21
  117.9 0.6 constant_dynamic-update-slice_fusion.20
  123.1 0.6 constant_dynamic-update-slice_fusion.11
  130.1 4.4 %all-to-all-start.2 = ((f32[64,4,1,128]{3,1,2,0:T(4,128)}), f32[64,4,1,128]{3,1,2,0:T(4,128)S(1)}, u32[]{:S(2)}, u32[]{:S(2)}) async-start(f32[64,4,1,128]{3,1,2,0:T(4,128)} %constant_dynamic-update-slice_fusion), calls=%async_computation.2 | async-start | bytes 262144 | tf_op jit(solution)/shard_map/all_to_all | solution.py:195
  134.6 4.1 %sine_multiply_fusion = (f32[512,1,512]{2,0,1:T(8,128)S(1)}, f32[512,1,512]{2,0,1:T(8,128)S(1)}) fusion(), kind=kLoop, calls=%fused_computation.37 | loop fusion | flops 3932160 | bytes 2097152 | tf_op jit(solution)/shard_map/mul | solution.py:74
  138.7 14.6 %all-to-all-done.2 = f32[64,4,1,128]{3,1,2,0:T(4,128)S(1)} async-done(((f32[64,4,1,128]{3,1,2,0:T(4,128)}), f32[64,4,1,128]{3,1,2,0:T(4,128)S(1)}, u32[]{:S(2)}, u32[]{:S(2)}) %all-to-all-start.2) | async-done | bytes 131104 | tf_op jit(solution)/shard_map/all_to_all | solution.py:195
  154.5 0.7 copy.47
  155.2 3.6 %all-to-all-start.3 = ((f32[4,64,128]{2,0,1:T(4,128)}), f32[4,64,128]{2,0,1:T(4,128)S(1)}, u32[]{:S(2)}, u32[]{:S(2)}) async-start(f32[4,64,128]{2,0,1:T(4,128)} %copy.47), calls=%async_computation.3 | async-start | bytes 262144 | tf_op jit(solution)/shard_map/all_to_all | solution.py:199
  159.0 3.0 %copy.49 = f32[512,2,512]{2,1,0:T(2,128)} copy(f32[512,2,512]{2,0,1:T(8,128)S(1)} %pad_maximum_fusion.1) | data formatting | bytes 4194304 | tf_op jit(solution)/shard_map/stack | solution.py:165
  162.0 2.7 %reshape.1428 = f32[1024,512]{1,0:T(8,128)S(1)} reshape(f32[512,2,512]{2,1,0:T(2,128)} %copy.49) | data formatting | bytes 4194304 | tf_op jit(solution)/shard_map/reshape | solution.py:165
  164.8 1.3 fusion.66
  166.1 2.7 %collective-permute-start.2 = (f32[3,8,512]{2,1,0:T(8,128)S(1)}, f32[3,8,512]{2,1,0:T(8,128)S(1)}, u32[]{:S(2)}, u32[]{:S(2)}) collective-permute-start(f32[3,8,512]{2,1,0:T(8,128)S(1)} %slice_bitcast_fusion), channel_id=1, source_target_pairs={{8,0},{16,8},{24,16},{32,24},{40,32},{48,40},{56,48},{64,56},{72,6... | collective-permute-start | bytes 147464 | tf_op jit(solution)/shard_map/ppermute | solution.py:18
  169.5 3.5 %collective-permute-done.2 = f32[3,8,512]{2,1,0:T(8,128)S(1)} collective-permute-done((f32[3,8,512]{2,1,0:T(8,128)S(1)}, f32[3,8,512]{2,1,0:T(8,128)S(1)}, u32[]{:S(2)}, u32[]{:S(2)}) %collective-permute-start.2) | collective-permute-done | bytes 49184 | tf_op jit(solution)/shard_map/ppermute | solution.py:18
  173.0 5.2 %collective-permute-start.3 = (f32[7,3,512]{2,1,0:T(4,128)S(1)}, f32[7,3,512]{2,1,0:T(4,128)S(1)}, u32[]{:S(2)}, u32[]{:S(2)}) collective-permute-start(f32[7,3,512]{2,1,0:T(4,128)S(1)} %pad_maximum_fusion.5), channel_id=1, source_target_pairs={{1,0},{2,1},{3,2},{4,3},{5,4},{6,5},{7,6},{0,7},{9,8},{10,9},{11,1... | collective-permute-start | bytes 129032 | tf_op jit(solution)/shard_map/ppermute | solution.py:18
  178.2 1.2 collective-permute-done.3
  179.4 1.2 multiply_reduce_fusion.1
  180.7 1.2 fusion.3
  182.5 0.6 maximum_multiply_fusion
  (106 shorter events, 38.0 us)
Async XLA Ops:
  5.2 11.6 %collective-permute-start = (f32[3,11,512]{2,1,0:T(8,128)S(1)}, f32[3,11,512]{2,1,0:T(8,128)S(1)}, u32[]{:S(2)}, u32[]{:S(2)}) collective-permute-start(f32[3,11,512]{2,1,0:T(8,128)S(1)} %slice.399), channel_id=1, source_target_pairs={{504,0},{0,8},{8,16},{16,24},{24,32},{32,40},{40,48},{48,56},{56,6... | collective-permute-start | bytes 202760 | tf_op jit(solution)/shard_map/ppermute | solution.py:18
  16.8 9.7 %collective-permute-start.1 = (f32[4,3,512]{2,1,0:T(4,128)S(1)}, f32[4,3,512]{2,1,0:T(4,128)S(1)}, u32[]{:S(2)}, u32[]{:S(2)}) collective-permute-start(f32[4,3,512]{2,1,0:T(4,128)S(1)} %slice.435), channel_id=1, source_target_pairs={{7,0},{0,1},{1,2},{2,3},{3,4},{4,5},{5,6},{6,7},{15,8},{8,9},{9,10... | collective-permute-start | bytes 73736 | tf_op jit(solution)/shard_map/ppermute | solution.py:18
  32.7 9.3 %all-to-all-start = ((f32[8,1,4096]{2,1,0:T(1,128)}), f32[8,1,4096]{2,1,0:T(1,128)S(1)}, u32[]{:S(2)}, u32[]{:S(2)}) async-start(f32[8,1,4096]{2,1,0:T(1,128)} %reshape.1437), calls=%async_computation | async-start | bytes 262144 | tf_op jit(solution)/shard_map/all_to_all | solution.py:179
  48.6 37.1 %all-to-all-start.1 = ((f32[4,64,128]{2,0,1:T(4,128)}), f32[4,64,128]{2,0,1:T(4,128)S(1)}, u32[]{:S(2)}, u32[]{:S(2)}) async-start(f32[4,64,128]{2,0,1:T(4,128)} %copy.43), calls=%async_computation.1 | async-start | bytes 262144 | tf_op jit(solution)/shard_map/all_to_all | solution.py:181
  130.1 23.1 %all-to-all-start.2 = ((f32[64,4,1,128]{3,1,2,0:T(4,128)}), f32[64,4,1,128]{3,1,2,0:T(4,128)S(1)}, u32[]{:S(2)}, u32[]{:S(2)}) async-start(f32[64,4,1,128]{3,1,2,0:T(4,128)} %constant_dynamic-update-slice_fusion), calls=%async_computation.2 | async-start | bytes 262144 | tf_op jit(solution)/shard_map/all_to_all | solution.py:195
  155.2 9.5 %all-to-all-start.3 = ((f32[4,64,128]{2,0,1:T(4,128)}), f32[4,64,128]{2,0,1:T(4,128)S(1)}, u32[]{:S(2)}, u32[]{:S(2)}) async-start(f32[4,64,128]{2,0,1:T(4,128)} %copy.47), calls=%async_computation.3 | async-start | bytes 262144 | tf_op jit(solution)/shard_map/all_to_all | solution.py:199
  164.7 13.5 %copy-start = (f32[1,1,512]{2,1,0:T(1,128)S(1)}, f32[1,1,512]{2,1,0:T(1,128)}, u32[]{:S(2)}) copy-start(f32[1,1,512]{2,1,0:T(1,128)} %param.11) | copy-start | bytes 6148
  166.1 6.9 %collective-permute-start.2 = (f32[3,8,512]{2,1,0:T(8,128)S(1)}, f32[3,8,512]{2,1,0:T(8,128)S(1)}, u32[]{:S(2)}, u32[]{:S(2)}) collective-permute-start(f32[3,8,512]{2,1,0:T(8,128)S(1)} %slice_bitcast_fusion), channel_id=1, source_target_pairs={{8,0},{16,8},{24,16},{32,24},{40,32},{48,40},{56,48},{64,56},{72,6... | collective-permute-start | bytes 147464 | tf_op jit(solution)/shard_map/ppermute | solution.py:18
  173.0 6.4 %collective-permute-start.3 = (f32[7,3,512]{2,1,0:T(4,128)S(1)}, f32[7,3,512]{2,1,0:T(4,128)S(1)}, u32[]{:S(2)}, u32[]{:S(2)}) collective-permute-start(f32[7,3,512]{2,1,0:T(4,128)S(1)} %pad_maximum_fusion.5), channel_id=1, source_target_pairs={{1,0},{2,1},{3,2},{4,3},{5,4},{6,5},{7,6},{0,7},{9,8},{10,9},{11,1... | collective-permute-start | bytes 129032 | tf_op jit(solution)/shard_map/ppermute | solution.py:18
